TPU v7x, 512 devices: a whole 4x8x8 slice. The times are simulated.
512 devices in a mesh: chain: 64 (over y, x, core), cols: 8 (over z).
Axes of the slice: x: 4, y: 8, z: 8, core: 2. Of those that a mesh axis runs over, the one named last changes fastest.
Arguments:
- start_vectors: float32 [1024, 256, 256], P('chain', 'cols'), may hold values from -6 to 6
- factors: float32 [1024, 256, 256], P('chain', 'cols'), may hold values from -1.2 to 1.2, as said below
Outputs:
- vectors: float32 [1024, 256, 256], P('chain', 'cols')
- log_growth: float32 [256], P('cols')
Inputs may be any that keep to these rules, and one draw needn't show every extreme that they name: `factors`: the factor blocks of the shifted operator; every product of consecutive factor blocks is bounded.
All inputs are finite; a program needn't handle non-finite values.
Results may differ from a plain program's by a relative error of at most 0.0003.
Values sent between devices are 32-bit elements; how exact they have to be, the bound alone decides.
No kernel may reach another device: no remote copies, remote signals or barrier semaphores. Data moves between devices by JAX's collectives and lax.ppermute only.
A program may use at most 128 MiB of HBM per device.

v0:
```python
import jax
import jax.numpy as jnp
from jax import lax
from jax.sharding import PartitionSpec as P

eps_value = 1e-06


def from_behind(block, axis, distance):
    devices = range(lax.axis_size(axis))
    route = [(i - distance, i) for i in devices if i - distance in devices]
    return lax.ppermute(block, axis, route)


def transform(matrix, vectors_in):
    return lax.dot_general(
        vectors_in,
        matrix,
        (((1,), (1,)), ((), ())),
        precision=lax.Precision.HIGHEST,
        preferred_element_type=jnp.float32,
    )


def compose(later, earlier):
    return jnp.dot(
        later, earlier, precision=lax.Precision.HIGHEST, preferred_element_type=jnp.float32
    )


def forward_rows(factors, right_side, incoming):

    def forward_advance(carried, element):
        matrix, source = element
        carried = transform(matrix, carried) + source
        return (carried, carried)

    return lax.scan(forward_advance, incoming, (factors, right_side))


def backward_rows(factors, forward, incoming):

    def backward_advance(carried, element):
        matrix, source = element
        carried = transform(matrix, source + carried)
        return (carried, carried)

    return lax.scan(backward_advance, incoming, (factors, forward), reverse=True)


def chain_operator(factors, reverse):
    identity_block = jnp.eye(factors.shape[1], dtype=jnp.float32)

    def chain_advance(running, matrix):
        return (compose(matrix, running), None)

    running, _ = lax.scan(chain_advance, identity_block, factors, reverse=reverse)
    return running


def section_count():
    return (lax.axis_size("chain") - 1).bit_length()


def enter_state(summary, direction):
    return from_behind(summary, "chain", direction)


def solve_system(factors, right_side, prefix_forward, prefix_backward):
    zero_state = jnp.zeros(right_side.shape[1:], jnp.float32)
    local_last, _ = forward_rows(factors, right_side, zero_state)
    incoming = enter_state(prefix_forward(local_last), 1)
    _, forward = forward_rows(factors, right_side, incoming)
    local_first, _ = backward_rows(factors, forward, zero_state)
    incoming_back = enter_state(prefix_backward(local_first), -1)
    _, solved = backward_rows(factors, forward, incoming_back)
    return solved


def shards(start_vectors, factors):
    full_factors = lax.all_gather(factors, "cols", axis=1, tiled=True)

    def pair_prefix(operator, summary, direction):
        sections = section_count()
        for section_index in range(sections):
            distance = direction * (1 << section_index)
            if section_index + 1 < sections:
                received_op, received_sum = from_behind((operator, summary), "chain", distance)
                summary = transform(operator, received_sum) + summary
                operator = compose(operator, received_op)
            else:
                received_sum = from_behind(summary, "chain", distance)
                summary = transform(operator, received_sum) + summary
        return summary

    def prefix_forward(summary):
        return pair_prefix(chain_operator(full_factors, False), summary, 1)

    def prefix_backward(summary):
        return pair_prefix(chain_operator(full_factors, True), summary, -1)

    cell_count = start_vectors.shape[0] * lax.axis_size("chain") * start_vectors.shape[2]
    first_solve = solve_system(full_factors, start_vectors, prefix_forward, prefix_backward)
    first_squares = lax.psum(jnp.sum(first_solve * first_solve, axis=(0, 2)), "chain")
    scale_one = jnp.sqrt(first_squares / cell_count + eps_value)
    second_solve = solve_system(
        full_factors, first_solve / scale_one[None, :, None], prefix_forward, prefix_backward
    )
    second_squares = lax.psum(jnp.sum(second_solve * second_solve, axis=(0, 2)), "chain")
    scale_two = jnp.sqrt(second_squares / cell_count + eps_value)
    result_vectors = second_solve / scale_two[None, :, None]
    return (result_vectors, jnp.log(scale_two))


def solution(mesh):
    return jax.shard_map(
        shards,
        mesh=mesh,
        in_specs=(P("chain", "cols", None), P("chain", "cols", None)),
        out_specs=(P("chain", "cols", None), P("cols")),
        check_vma=False,
    )
```

profile of v0, /device:TPU:32, one launch (start us, length us, event | category | flops | bytes accessed | tf_op | source)
XLA Modules:
  0.0 812.4 jit_solution(6026892274242298097)
XLA Ops:
  8.0 64.7 %all-gather.2.cloned.1.call-done = f32[16,256,256]{2,1,0:T(8,128)} async-done(((f32[16,32,256]{2,1,0:T(8,128)}), f32[16,256,256]{2,1,0:T(8,128)}) %all-gather.2.cloned.1.call-update) | async-done | bytes 4194320 | tf_op jit(solution)/shard_map/all_gather | solution.py:81
  72.7 21.4 %while.146 = (s32[]{:T(128)}, f32[32,256]{1,0:T(8,128)S(1)}, f32[16,256,256]{2,1,0:T(8,128)}, f32[16,32,256]{2,1,0:T(8,128)}, s32[]{:T(128)}, /*index=5*/s32[]{:T(128)}) while((s32[]{:T(128)}, f32[32,256]{1,0:T(8,128)S(1)}, f32[16,256,256]{2,1,0:T(8,128)}, f32[16,32,256]{2,1,0:T(8,128)}, s32[]{:T(128)}, /*index=5*/s32[]{:T(128)}) %tuple.241), condition=%wide.region_1.2_spmd.clone, body=%wide.region_0.1_spmd.clone.sunk | while | flops 25182212 | bytes 427087 | solution.py:38
  94.1 1.9 collective-permute-start
  96.0 22.1 %while.138 = (s32[]{:T(128)}, f32[256,256]{1,0:T(8,128)S(1)}, f32[16,256,256]{2,1,0:T(8,128)}, s32[]{:T(128)}) while((s32[]{:T(128)}, f32[256,256]{1,0:T(8,128)S(1)}, f32[16,256,256]{2,1,0:T(8,128)}, s32[]{:T(128)}) %tuple.273), condition=%wide.region_3.4_spmd, body=%wide.region_2.3_spmd.sunk | while | flops 201326592 | bytes 1311285 | solution.py:57
  118.1 3.5 collective-permute-start.2
  122.0 3.4 collective-permute-start.1
  125.4 3.8 collective-permute-done.2
  131.8 2.7 collective-permute-start.3
  134.6 7.3 collective-permute-done.4
  144.5 1.9 collective-permute-start.5
  146.4 10.8 %collective-permute-done.6 = f32[256,256]{1,0:T(8,128)S(1)} collective-permute-done((f32[256,256]{1,0:T(8,128)S(1)}, f32[256,256]{1,0:T(8,128)S(1)}, u32[]{:S(2)}, u32[]{:S(2)}) %collective-permute-start.6) | collective-permute-done | bytes 262176 | tf_op jit(solution)/shard_map/ppermute | solution.py:12
  161.9 7.5 collective-permute-done.8
  169.7 1.9 collective-permute-start.10
  173.3 7.5 collective-permute-done.10
  184.0 6.6 collective-permute-done.11
  190.7 21.4 %while.139 = (s32[]{:T(128)}, f32[32,256]{1,0:T(8,128)S(1)}, f32[16,32,256]{2,1,0:T(8,128)S(1)}, f32[16,256,256]{2,1,0:T(8,128)}, f32[16,32,256]{2,1,0:T(8,128)}, /*index=5*/s32[]{:T(128)}) while((s32[]{:T(128)}, f32[32,256]{1,0:T(8,128)S(1)}, f32[16,32,256]{2,1,0:T(8,128)S(1)}, f32[16,256,256]{2,1,0:T(8,128)}, f32[16,32,256]{2,1,0:T(8,128)}, ...), condition=%wide.region_5.6_spmd, body=%wide.region_4.5_spmd.sunk | while | flops 25174016 | bytes 459845 | solution.py:38
  212.1 21.3 %while.140 = (s32[]{:T(128)}, f32[32,256]{1,0:T(8,128)S(1)}, f32[16,32,256]{2,1,0:T(8,128)S(1)}, f32[16,256,256]{2,1,0:T(8,128)}, s32[]{:T(128)}, /*index=5*/s32[]{:T(128)}) while((s32[]{:T(128)}, f32[32,256]{1,0:T(8,128)S(1)}, f32[16,32,256]{2,1,0:T(8,128)S(1)}, f32[16,256,256]{2,1,0:T(8,128)}, s32[]{:T(128)}, /*index=5*/s32[]{:T(128)}) %tuple.275), condition=%wide.region_7.8_spmd, body=%wide.region_6.7_spmd.sunk | while | flops 25174020 | bytes 427089 | solution.py:48
  235.4 22.1 %while.141 = (s32[]{:T(128)}, f32[256,256]{1,0:T(8,128)S(1)}, f32[16,256,256]{2,1,0:T(8,128)}, s32[]{:T(128)}, s32[]{:T(128)}) while((s32[]{:T(128)}, f32[256,256]{1,0:T(8,128)S(1)}, f32[16,256,256]{2,1,0:T(8,128)}, s32[]{:T(128)}, s32[]{:T(128)}) %tuple.276), condition=%wide.region_9.10_spmd, body=%wide.region_8.9_spmd.sunk | while | flops 201326592 | bytes 1310797 | solution.py:57
  259.8 1.9 collective-permute-start.13
  261.8 1.9 collective-permute-done.14
  264.1 1.9 collective-permute-start.16
  266.9 4.4 collective-permute-start.15
  271.4 2.5 collective-permute-done.16
  278.5 7.5 collective-permute-done.18
  286.3 2.1 collective-permute-start.20
  290.7 6.7 collective-permute-done.20
  301.4 13.4 %collective-permute-done.22 = f32[256,256]{1,0:T(8,128)S(1)} collective-permute-done((f32[256,256]{1,0:T(8,128)S(1)}, f32[256,256]{1,0:T(8,128)S(1)}, u32[]{:S(2)}, u32[]{:S(2)}) %collective-permute-start.22) | collective-permute-done | bytes 262176 | tf_op jit(solution)/shard_map/ppermute | solution.py:12
  315.6 5.5 collective-permute-start.23
  322.7 21.6 %while.142 = (s32[]{:T(128)}, f32[32,256]{1,0:T(8,128)S(1)}, f32[16,32,256]{2,1,0:T(8,128)S(1)}, f32[16,32,256]{2,1,0:T(8,128)}, f32[16,256,256]{2,1,0:T(8,128)}, /*index=5*/s32[]{:T(128)}, s32[]{:T(128)}) while((s32[]{:T(128)}, f32[32,256]{1,0:T(8,128)S(1)}, f32[16,32,256]{2,1,0:T(8,128)S(1)}, f32[16,32,256]{2,1,0:T(8,128)}, ...), condition=%wide.region_11.12_spmd, body=%wide.region_10.11_spmd.sunk | while | flops 25174020 | bytes 460377 | solution.py:48
  344.5 129.1 %psum.14 = f32[32]{0:T(128)S(1)} all-reduce(f32[32]{0:T(128)S(1)} %multiply_reduce_fusion.1), channel_id=1, replica_groups=mesh['chain'=64,'cols'=8] {'chain'}, use_global_device_ids=true, to_apply=%region_13.14 | all-reduce | flops 32 | bytes 256 | tf_op jit(solution)/shard_map/psum | solution.py:104
  474.5 21.5 %while.147 = (s32[]{:T(128)}, f32[32,256]{1,0:T(8,128)S(1)}, f32[16,256,256]{2,1,0:T(8,128)}, f32[16,32,256]{2,1,0:T(8,128)}, s32[]{:T(128)}, /*index=5*/s32[]{:T(128)}) while((s32[]{:T(128)}, f32[32,256]{1,0:T(8,128)S(1)}, f32[16,256,256]{2,1,0:T(8,128)}, f32[16,32,256]{2,1,0:T(8,128)}, s32[]{:T(128)}, ...), condition=%wide.region_15.16_spmd.clone, body=%wide.region_14.15_spmd.clone.sunk | while | flops 25182212 | bytes 427087 | solution.py:38
  497.9 6.6 collective-permute-done.24
  506.8 7.2 collective-permute-done.25
  514.4 2.1 collective-permute-start.26
  516.4 7.5 collective-permute-done.26
  526.2 5.1 collective-permute-done.27
  533.6 6.0 collective-permute-done.28
  541.4 8.2 %collective-permute-done.29 = f32[32,256]{1,0:T(8,128)S(1)} collective-permute-done((f32[32,256]{1,0:T(8,128)S(1)}, f32[32,256]{1,0:T(8,128)S(1)}, u32[]{:S(2)}, u32[]{:S(2)}) %collective-permute-start.29) | collective-permute-done | bytes 32800 | tf_op jit(solution)/shard_map/ppermute | solution.py:12
  551.9 6.6 collective-permute-done.30
  558.6 21.4 %while.143 = (s32[]{:T(128)}, f32[32,256]{1,0:T(8,128)S(1)}, f32[16,32,256]{2,1,0:T(8,128)S(1)}, f32[16,256,256]{2,1,0:T(8,128)}, f32[16,32,256]{2,1,0:T(8,128)}, /*index=5*/s32[]{:T(128)}) while((s32[]{:T(128)}, f32[32,256]{1,0:T(8,128)S(1)}, f32[16,32,256]{2,1,0:T(8,128)S(1)}, f32[16,256,256]{2,1,0:T(8,128)}, f32[16,32,256]{2,1,0:T(8,128)}, ...), condition=%wide.region_17.18_spmd, body=%wide.region_16.17_spmd.sunk | while | flops 25174016 | bytes 459845 | solution.py:38
  580.0 21.3 %while.144 = (s32[]{:T(128)}, f32[32,256]{1,0:T(8,128)S(1)}, f32[16,32,256]{2,1,0:T(8,128)S(1)}, f32[16,256,256]{2,1,0:T(8,128)}, s32[]{:T(128)}, /*index=5*/s32[]{:T(128)}) while((s32[]{:T(128)}, f32[32,256]{1,0:T(8,128)S(1)}, f32[16,32,256]{2,1,0:T(8,128)S(1)}, f32[16,256,256]{2,1,0:T(8,128)}, s32[]{:T(128)}, /*index=5*/s32[]{:T(128)}) %tuple.280), condition=%wide.region_19.20_spmd, body=%wide.region_18.19_spmd.sunk | while | flops 25174020 | bytes 427089 | solution.py:48
  607.1 3.9 collective-permute-done.32
  613.3 5.4 collective-permute-done.33
  620.9 4.1 collective-permute-done.34
  627.3 4.8 collective-permute-done.35
  635.6 16.2 %collective-permute-start.37 = (f32[32,256]{1,0:T(8,128)S(1)}, f32[32,256]{1,0:T(8,128)S(1)}, u32[]{:S(2)}, u32[]{:S(2)}) collective-permute-start(f32[32,256]{1,0:T(8,128)S(1)} %convolution_add_fusion), channel_id=1, source_target_pairs={{8,0},{16,8},{24,16},{32,24},{40,32},{48,40},{56,48},{64,56},{72,6... | collective-permute-start | bytes 98312 | tf_op jit(solution)/shard_map/ppermute | solution.py:12
  653.5 21.3 %while.145 = (s32[]{:T(128)}, f32[32,256]{1,0:T(8,128)S(1)}, f32[16,32,256]{2,1,0:T(8,128)S(1)}, f32[16,32,256]{2,1,0:T(8,128)S(1)}, f32[16,256,256]{2,1,0:T(8,128)}, /*index=5*/s32[]{:T(128)}, s32[]{:T(128)}) while((s32[]{:T(128)}, f32[32,256]{1,0:T(8,128)S(1)}, f32[16,32,256]{2,1,0:T(8,128)S(1)}, f32[16,32,256]{2,1,0:T(8,128)S(1)}, ...), condition=%wide.region_21.22_spmd, body=%wide.region_20.21_spmd.sunk | while | flops 25174020 | bytes 460377 | solution.py:48
  675.0 129.1 %psum.15 = f32[32]{0:T(128)S(1)} all-reduce(f32[32]{0:T(128)S(1)} %multiply_reduce_fusion), channel_id=1, replica_groups=mesh['chain'=64,'cols'=8] {'chain'}, use_global_device_ids=true, to_apply=%region_23.24 | all-reduce | flops 32 | bytes 256 | tf_op jit(solution)/shard_map/psum | solution.py:109
  (419 shorter events, 279.4 us)
Async XLA Ops:
  7.2 65.5 %all-gather.2.cloned.1.call-start = ((), (), s32[]{:S(2)}) async-start(), calls=%async_computation | async-start | bytes 4718592 | tf_op jit(solution)/shard_map/all_gather | solution.py:81
  94.1 27.5 %collective-permute-start = (f32[32,256]{1,0:T(8,128)S(1)}, f32[32,256]{1,0:T(8,128)S(1)}, u32[]{:S(2)}, u32[]{:S(2)}) collective-permute-start(f32[32,256]{1,0:T(8,128)S(1)} %get-tuple-element.568), channel_id=1, source_target_pairs={{0,8},{8,16},{16,24},{24,32},{32,40},{40,48},{48,56},{56,64},{64,7... | collective-permute-start | bytes 98312 | tf_op jit(solution)/shard_map/ppermute | solution.py:12
  118.1 11.0 %collective-permute-start.2 = (f32[256,256]{1,0:T(8,128)S(1)}, f32[256,256]{1,0:T(8,128)S(1)}, u32[]{:S(2)}, u32[]{:S(2)}) collective-permute-start(f32[256,256]{1,0:T(8,128)S(1)} %get-tuple-element.569), channel_id=1, source_target_pairs={{0,8},{8,16},{16,24},{24,32},{32,40},{40,48},{48,56},{56,64},{64,7... | collective-permute-start | bytes 786440 | tf_op jit(solution)/shard_map/ppermute | solution.py:12
  122.0 9.5 %collective-permute-start.1 = (f32[32,256]{1,0:T(8,128)S(1)}, f32[32,256]{1,0:T(8,128)S(1)}, u32[]{:S(2)}, u32[]{:S(2)}) collective-permute-start(f32[32,256]{1,0:T(8,128)S(1)} %convolution_add_fusion.23), channel_id=1, source_target_pairs={{0,16},{8,24},{16,32},{24,40},{32,48},{40,56},{48,64},{56,72},{64,... | collective-permute-start | bytes 98312 | tf_op jit(solution)/shard_map/ppermute | solution.py:12
  129.5 12.3 %collective-permute-start.4 = (f32[256,256]{1,0:T(8,128)S(1)}, f32[256,256]{1,0:T(8,128)S(1)}, u32[]{:S(2)}, u32[]{:S(2)}) collective-permute-start(f32[256,256]{1,0:T(8,128)S(1)} %fusion.54), channel_id=1, source_target_pairs={{0,16},{8,24},{16,32},{24,40},{32,48},{40,56},{48,64},{56,72},{64,... | collective-permute-start | bytes 786440 | tf_op jit(solution)/shard_map/ppermute | solution.py:12
  131.8 12.3 %collective-permute-start.3 = (f32[32,256]{1,0:T(8,128)S(1)}, f32[32,256]{1,0:T(8,128)S(1)}, u32[]{:S(2)}, u32[]{:S(2)}) collective-permute-start(f32[32,256]{1,0:T(8,128)S(1)} %convolution_add_fusion.22), channel_id=1, source_target_pairs={{0,32},{8,40},{16,48},{24,56},{32,64},{40,72},{48,80},{56,88},{64,... | collective-permute-start | bytes 98312 | tf_op jit(solution)/shard_map/ppermute | solution.py:12
  142.2 15.0 %collective-permute-start.6 = (f32[256,256]{1,0:T(8,128)S(1)}, f32[256,256]{1,0:T(8,128)S(1)}, u32[]{:S(2)}, u32[]{:S(2)}) collective-permute-start(f32[256,256]{1,0:T(8,128)S(1)} %fusion.55), channel_id=1, source_target_pairs={{0,32},{8,40},{16,48},{24,56},{32,64},{40,72},{48,80},{56,88},{64,... | collective-permute-start | bytes 786440 | tf_op jit(solution)/shard_map/ppermute | solution.py:12
  144.5 15.1 %collective-permute-start.5 = (f32[32,256]{1,0:T(8,128)S(1)}, f32[32,256]{1,0:T(8,128)S(1)}, u32[]{:S(2)}, u32[]{:S(2)}) collective-permute-start(f32[32,256]{1,0:T(8,128)S(1)} %convolution_add_fusion.21), channel_id=1, source_target_pairs={{0,64},{8,72},{16,80},{24,88},{32,96},{40,104},{48,112},{56,120},{... | collective-permute-start | bytes 98312 | tf_op jit(solution)/shard_map/ppermute | solution.py:12
  157.6 11.7 %collective-permute-start.8 = (f32[256,256]{1,0:T(8,128)S(1)}, f32[256,256]{1,0:T(8,128)S(1)}, u32[]{:S(2)}, u32[]{:S(2)}) collective-permute-start(f32[256,256]{1,0:T(8,128)S(1)} %fusion.56), channel_id=1, source_target_pairs={{0,64},{8,72},{16,80},{24,88},{32,96},{40,104},{48,112},{56,120},{... | collective-permute-start | bytes 786440 | tf_op jit(solution)/shard_map/ppermute | solution.py:12
  159.9 11.7 %collective-permute-start.7 = (f32[32,256]{1,0:T(8,128)S(1)}, f32[32,256]{1,0:T(8,128)S(1)}, u32[]{:S(2)}, u32[]{:S(2)}) collective-permute-start(f32[32,256]{1,0:T(8,128)S(1)} %convolution_add_fusion.20), channel_id=1, source_target_pairs={{0,128},{8,136},{16,144},{24,152},{32,160},{40,168},{48,176},{56,1... | collective-permute-start | bytes 98312 | tf_op jit(solution)/shard_map/ppermute | solution.py:12
  169.7 11.1 %collective-permute-start.10 = (f32[256,256]{1,0:T(8,128)S(1)}, f32[256,256]{1,0:T(8,128)S(1)}, u32[]{:S(2)}, u32[]{:S(2)}) collective-permute-start(f32[256,256]{1,0:T(8,128)S(1)} %fusion.57), channel_id=1, source_target_pairs={{0,128},{8,136},{16,144},{24,152},{32,160},{40,168},{48,176},{56,1... | collective-permute-start | bytes 786440 | tf_op jit(solution)/shard_map/ppermute | solution.py:12
  172.0 9.7 %collective-permute-start.9 = (f32[32,256]{1,0:T(8,128)S(1)}, f32[32,256]{1,0:T(8,128)S(1)}, u32[]{:S(2)}, u32[]{:S(2)}) collective-permute-start(f32[32,256]{1,0:T(8,128)S(1)} %convolution_add_fusion.19), channel_id=1, source_target_pairs={{0,256},{8,264},{16,272},{24,280},{32,288},{40,296},{48,304},{56,3... | collective-permute-start | bytes 98312 | tf_op jit(solution)/shard_map/ppermute | solution.py:12
  182.1 8.6 %collective-permute-start.11 = (f32[32,256]{1,0:T(8,128)S(1)}, f32[32,256]{1,0:T(8,128)S(1)}, u32[]{:S(2)}, u32[]{:S(2)}) collective-permute-start(f32[32,256]{1,0:T(8,128)S(1)} %convolution_add_fusion.18), channel_id=1, source_target_pairs={{0,8},{8,16},{16,24},{24,32},{32,40},{40,48},{48,56},{56,64},{64,7... | collective-permute-start | bytes 98312 | tf_op jit(solution)/shard_map/ppermute | solution.py:12
  233.4 28.3 %copy-start.2 = (f32[16,32,256]{2,1,0:T(8,128)}, f32[16,32,256]{2,1,0:T(8,128)S(1)}, u32[]{:S(2)}) copy-start(f32[16,32,256]{2,1,0:T(8,128)S(1)} %get-tuple-element.1180) | copy-start | bytes 1572868
  233.5 26.0 %collective-permute-start.12 = (f32[32,256]{1,0:T(8,128)S(1)}, f32[32,256]{1,0:T(8,128)S(1)}, u32[]{:S(2)}, u32[]{:S(2)}) collective-permute-start(f32[32,256]{1,0:T(8,128)S(1)} %get-tuple-element.571), channel_id=1, source_target_pairs={{8,0},{16,8},{24,16},{32,24},{40,32},{48,40},{56,48},{64,56},{72,6... | collective-permute-start | bytes 98312 | tf_op jit(solution)/shard_map/ppermute | solution.py:12
  257.5 6.1 collective-permute-start.14
  259.8 6.8 collective-permute-start.13
  264.1 9.8 %collective-permute-start.16 = (f32[256,256]{1,0:T(8,128)S(1)}, f32[256,256]{1,0:T(8,128)S(1)}, u32[]{:S(2)}, u32[]{:S(2)}) collective-permute-start(f32[256,256]{1,0:T(8,128)S(1)} %fusion.59), channel_id=1, source_target_pairs={{16,0},{24,8},{32,16},{40,24},{48,32},{56,40},{64,48},{72,56},{80,... | collective-permute-start | bytes 786440 | tf_op jit(solution)/shard_map/ppermute | solution.py:12
  266.9 9.2 %collective-permute-start.15 = (f32[32,256]{1,0:T(8,128)S(1)}, f32[32,256]{1,0:T(8,128)S(1)}, u32[]{:S(2)}, u32[]{:S(2)}) collective-permute-start(f32[32,256]{1,0:T(8,128)S(1)} %convolution_add_fusion.16), channel_id=1, source_target_pairs={{32,0},{40,8},{48,16},{56,24},{64,32},{72,40},{80,48},{88,56},{96,... | collective-permute-start | bytes 98312 | tf_op jit(solution)/shard_map/ppermute | solution.py:12
  274.3 11.7 %collective-permute-start.18 = (f32[256,256]{1,0:T(8,128)S(1)}, f32[256,256]{1,0:T(8,128)S(1)}, u32[]{:S(2)}, u32[]{:S(2)}) collective-permute-start(f32[256,256]{1,0:T(8,128)S(1)} %fusion.60), channel_id=1, source_target_pairs={{32,0},{40,8},{48,16},{56,24},{64,32},{72,40},{80,48},{88,56},{96,... | collective-permute-start | bytes 786440 | tf_op jit(solution)/shard_map/ppermute | solution.py:12
  276.5 11.9 %collective-permute-start.17 = (f32[32,256]{1,0:T(8,128)S(1)}, f32[32,256]{1,0:T(8,128)S(1)}, u32[]{:S(2)}, u32[]{:S(2)}) collective-permute-start(f32[32,256]{1,0:T(8,128)S(1)} %convolution_add_fusion.15), channel_id=1, source_target_pairs={{64,0},{72,8},{80,16},{88,24},{96,32},{104,40},{112,48},{120,56},{... | collective-permute-start | bytes 98312 | tf_op jit(solution)/shard_map/ppermute | solution.py:12
  286.3 11.1 %collective-permute-start.20 = (f32[256,256]{1,0:T(8,128)S(1)}, f32[256,256]{1,0:T(8,128)S(1)}, u32[]{:S(2)}, u32[]{:S(2)}) collective-permute-start(f32[256,256]{1,0:T(8,128)S(1)} %fusion.61), channel_id=1, source_target_pairs={{64,0},{72,8},{80,16},{88,24},{96,32},{104,40},{112,48},{120,56},{... | collective-permute-start | bytes 786440 | tf_op jit(solution)/shard_map/ppermute | solution.py:12
  288.8 11.0 %collective-permute-start.19 = (f32[32,256]{1,0:T(8,128)S(1)}, f32[32,256]{1,0:T(8,128)S(1)}, u32[]{:S(2)}, u32[]{:S(2)}) collective-permute-start(f32[32,256]{1,0:T(8,128)S(1)} %convolution_add_fusion.14), channel_id=1, source_target_pairs={{128,0},{136,8},{144,16},{152,24},{160,32},{168,40},{176,48},{184,... | collective-permute-start | bytes 98312 | tf_op jit(solution)/shard_map/ppermute | solution.py:12
  297.8 17.0 %collective-permute-start.22 = (f32[256,256]{1,0:T(8,128)S(1)}, f32[256,256]{1,0:T(8,128)S(1)}, u32[]{:S(2)}, u32[]{:S(2)}) collective-permute-start(f32[256,256]{1,0:T(8,128)S(1)} %fusion.62), channel_id=1, source_target_pairs={{128,0},{136,8},{144,16},{152,24},{160,32},{168,40},{176,48},{184,... | collective-permute-start | bytes 786440 | tf_op jit(solution)/shard_map/ppermute | solution.py:12
  300.1 15.1 %collective-permute-start.21 = (f32[32,256]{1,0:T(8,128)S(1)}, f32[32,256]{1,0:T(8,128)S(1)}, u32[]{:S(2)}, u32[]{:S(2)}) collective-permute-start(f32[32,256]{1,0:T(8,128)S(1)} %convolution_add_fusion.13), channel_id=1, source_target_pairs={{256,0},{264,8},{272,16},{280,24},{288,32},{296,40},{304,48},{312,... | collective-permute-start | bytes 98312 | tf_op jit(solution)/shard_map/ppermute | solution.py:12
  315.2 5.9 copy-start
  315.6 7.1 collective-permute-start.23
  496.0 8.6 %collective-permute-start.24 = (f32[32,256]{1,0:T(8,128)S(1)}, f32[32,256]{1,0:T(8,128)S(1)}, u32[]{:S(2)}, u32[]{:S(2)}) collective-permute-start(f32[32,256]{1,0:T(8,128)S(1)} %get-tuple-element.574), channel_id=1, source_target_pairs={{0,8},{8,16},{16,24},{24,32},{32,40},{40,48},{48,56},{56,64},{64,7... | collective-permute-start | bytes 98312 | tf_op jit(solution)/shard_map/ppermute | solution.py:12
  504.9 9.1 %collective-permute-start.25 = (f32[32,256]{1,0:T(8,128)S(1)}, f32[32,256]{1,0:T(8,128)S(1)}, u32[]{:S(2)}, u32[]{:S(2)}) collective-permute-start(f32[32,256]{1,0:T(8,128)S(1)} %convolution_add_fusion.11), channel_id=1, source_target_pairs={{0,16},{8,24},{16,32},{24,40},{32,48},{40,56},{48,64},{56,72},{64,... | collective-permute-start | bytes 98312 | tf_op jit(solution)/shard_map/ppermute | solution.py:12
  514.4 120.9 %copy-start.1 = (f32[256,256]{1,0:T(8,128)S(1)}, f32[256,256]{1,0:T(8,128)}, u32[]{:S(2)}) copy-start(f32[256,256]{1,0:T(8,128)} %copy-done) | copy-start | bytes 786436
  514.4 9.6 %collective-permute-start.26 = (f32[32,256]{1,0:T(8,128)S(1)}, f32[32,256]{1,0:T(8,128)S(1)}, u32[]{:S(2)}, u32[]{:S(2)}) collective-permute-start(f32[32,256]{1,0:T(8,128)S(1)} %convolution_add_fusion.10), channel_id=1, source_target_pairs={{0,32},{8,40},{16,48},{24,56},{32,64},{40,72},{48,80},{56,88},{64,... | collective-permute-start | bytes 98312 | tf_op jit(solution)/shard_map/ppermute | solution.py:12
  524.3 7.0 collective-permute-start.27
  531.6 7.9 collective-permute-start.28
  539.9 9.7 %collective-permute-start.29 = (f32[32,256]{1,0:T(8,128)S(1)}, f32[32,256]{1,0:T(8,128)S(1)}, u32[]{:S(2)}, u32[]{:S(2)}) collective-permute-start(f32[32,256]{1,0:T(8,128)S(1)} %convolution_add_fusion.7), channel_id=1, source_target_pairs={{0,256},{8,264},{16,272},{24,280},{32,288},{40,296},{48,304},{56,3... | collective-permute-start | bytes 98312 | tf_op jit(solution)/shard_map/ppermute | solution.py:12
  550.0 8.6 %collective-permute-start.30 = (f32[32,256]{1,0:T(8,128)S(1)}, f32[32,256]{1,0:T(8,128)S(1)}, u32[]{:S(2)}, u32[]{:S(2)}) collective-permute-start(f32[32,256]{1,0:T(8,128)S(1)} %convolution_add_fusion.6), channel_id=1, source_target_pairs={{0,8},{8,16},{16,24},{24,32},{32,40},{40,48},{48,56},{56,64},{64,7... | collective-permute-start | bytes 98312 | tf_op jit(solution)/shard_map/ppermute | solution.py:12
  601.3 3.5 collective-permute-start.31
  605.2 5.8 collective-permute-start.32
  611.3 7.3 collective-permute-start.33
  619.0 6.0 collective-permute-start.34
  625.3 6.7 collective-permute-start.35
  632.4 2.9 collective-permute-start.36
  635.6 17.8 %collective-permute-start.37 = (f32[32,256]{1,0:T(8,128)S(1)}, f32[32,256]{1,0:T(8,128)S(1)}, u32[]{:S(2)}, u32[]{:S(2)}) collective-permute-start(f32[32,256]{1,0:T(8,128)S(1)} %convolution_add_fusion), channel_id=1, source_target_pairs={{8,0},{16,8},{24,16},{32,24},{40,32},{48,40},{56,48},{64,56},{72,6... | collective-permute-start | bytes 98312 | tf_op jit(solution)/shard_map/ppermute | solution.py:12
Sparse Core Ops, SparseCore 0:
  10.1 62.5 all-gather.1
where the time goes:
time: 818 us; the launch traced here: 812 us
  blocking collectives  258 us (32%)
  matrix products  221 us (27%)
  waiting for transfers between devices  214 us (26%)
  starting transfers between devices  95.2 us (12%)
  between operations  14.9 us (2%)
    dot_general x152, matrix products, transform(): lax.dot_general(vectors_in, matrix, (((1,), (1,)), ((), ())), precision=l...  175 us
    ppermute x38, waiting for transfers between devices, from_behind(): return lax.ppermute(block, axis, route)  148 us
    psum x1, blocking collectives, shards(): lax.psum(jnp.sum(second_solve * second_solve, axis=(0, 2)), 'chain')  129 us
    psum x1, blocking collectives, shards(): lax.psum(jnp.sum(first_solve * first_solve, axis=(0, 2)), 'chain')  129 us
    ppermute x38, starting transfers between devices, from_behind(): return lax.ppermute(block, axis, route)  95.2 us
    all_gather x1, waiting for transfers between devices, shards(): full_factors = lax.all_gather(factors, 'cols', axis=1, tiled=True)  64.7 us
    dot_general x42, matrix products, compose(): jnp.dot(later, earlier, precision=lax.Precision.HIGHEST, preferred_elemen...  46.4 us
  transfers between devices with their start and end apart: 39, of which 29 were waited for; matrix products, arithmetic and copies ran while one was open for 6% of the time, Pallas kernels for 0%

commit v1 on v0

--- a/solution.py
+++ b/solution.py
@@ -78,7 +78,11 @@
 
 
 def shards(start_vectors, factors):
-    full_factors = lax.all_gather(factors, "cols", axis=1, tiled=True)
+    devices_2 = lax.axis_size("cols")
+    repeats = [devices_2 if d == 1 else 1 for d in range(factors.ndim)]
+    full_factors = lax.all_to_all(
+        jnp.tile(factors, repeats), "cols", split_axis=1, concat_axis=1, tiled=True
+    )
 
     def pair_prefix(operator, summary, direction):
         sections = section_count()

time: 818 us -> 853 us (1.043)
  waiting for transfers between devices: 214 us -> 244 us
  between operations: 14.9 us -> 1.48 us
  local copies, waits for them, and re-layouts: 1.35 us -> 12.5 us
    all_to_all x0 -> x1, waiting for transfers between devices: none -> 96.2 us  [shards(): lax.all_to_all(jnp.tile(factors, repeats), 'cols', split_axis=1, concat_a...]
    all_gather x1 -> x0, waiting for transfers between devices: 64.7 us -> none  [shards(): full_factors = lax.all_gather(factors, 'cols', axis=1, tiled=True)]
    all_to_all x0 -> x1, starting transfers between devices: none -> 10.3 us  [shards(): lax.all_to_all(jnp.tile(factors, repeats), 'cols', split_axis=1, concat_a...]
    unnamed x7 -> x9, local copies, waits for them, and re-layouts: 0.03 us -> 8.66 us
where the time goes in v1:
time: 853 us; the launch traced here: 848 us
  blocking collectives  258 us (30%)
  waiting for transfers between devices  244 us (29%)
  matrix products  221 us (26%)
  starting transfers between devices  102 us (12%)
  local copies, waits for them, and re-layouts  12.5 us (1%)
    dot_general x152, matrix products, transform(): lax.dot_general(vectors_in, matrix, (((1,), (1,)), ((), ())), precision=l...  175 us
    ppermute x38, waiting for transfers between devices, from_behind(): return lax.ppermute(block, axis, route)  148 us
    psum x1, blocking collectives, shards(): lax.psum(jnp.sum(second_solve * second_solve, axis=(0, 2)), 'chain')  129 us
    psum x1, blocking collectives, shards(): lax.psum(jnp.sum(first_solve * first_solve, axis=(0, 2)), 'chain')  129 us
    all_to_all x1, waiting for transfers between devices, shards(): lax.all_to_all(jnp.tile(factors, repeats), 'cols', split_axis=1, concat_a...  96.2 us
    ppermute x38, starting transfers between devices, from_behind(): return lax.ppermute(block, axis, route)  91.9 us
    dot_general x42, matrix products, compose(): jnp.dot(later, earlier, precision=lax.Precision.HIGHEST, preferred_elemen...  46.4 us
  transfers between devices with their start and end apart: 39, of which 29 were waited for; matrix products, arithmetic and copies ran while one was open for 6% of the time, Pallas kernels for 0%

profile of v1, /device:TPU:32, one launch (start us, length us, event | category | flops | bytes accessed | tf_op | source)
XLA Modules:
  0.0 847.9 jit_solution(10913627962332387379)
XLA Ops:
  2.0 2.5 tile.4
  4.5 10.3 %all-to-all-start = ((f32[16,256,256]{2,0,1:T(8,128)}), f32[16,256,256]{2,0,1:T(8,128)}, u32[]{:S(2)}, u32[]{:S(2)}) async-start(f32[16,256,256]{2,0,1:T(8,128)} %bitcast.211), calls=%async_computation | async-start | bytes 8388608 | tf_op jit(solution)/shard_map/all_to_all | solution.py:83
  14.8 96.2 %all-to-all-done = f32[16,256,256]{2,0,1:T(8,128)} async-done(((f32[16,256,256]{2,0,1:T(8,128)}), f32[16,256,256]{2,0,1:T(8,128)}, u32[]{:S(2)}, u32[]{:S(2)}) %all-to-all-start) | async-done | bytes 4194336 | tf_op jit(solution)/shard_map/all_to_all | solution.py:83
  111.0 6.6 copy.11
  117.6 21.4 %while.146 = (s32[]{:T(128)}, f32[32,256]{1,0:T(8,128)S(1)}, f32[16,256,256]{2,1,0:T(8,128)}, f32[16,32,256]{2,1,0:T(8,128)}, s32[]{:T(128)}, /*index=5*/s32[]{:T(128)}) while((s32[]{:T(128)}, f32[32,256]{1,0:T(8,128)S(1)}, f32[16,256,256]{2,1,0:T(8,128)}, f32[16,32,256]{2,1,0:T(8,128)}, s32[]{:T(128)}, /*index=5*/s32[]{:T(128)}) %tuple.251), condition=%wide.region_1.2_spmd.clone, body=%wide.region_0.1_spmd.clone.sunk | while | flops 25182212 | bytes 427087 | solution.py:38
  139.0 1.9 collective-permute-start
  141.0 22.1 %while.138 = (s32[]{:T(128)}, f32[256,256]{1,0:T(8,128)S(1)}, f32[16,256,256]{2,1,0:T(8,128)}, s32[]{:T(128)}) while((s32[]{:T(128)}, f32[256,256]{1,0:T(8,128)S(1)}, f32[16,256,256]{2,1,0:T(8,128)}, s32[]{:T(128)}) %tuple.281), condition=%wide.region_3.4_spmd, body=%wide.region_2.3_spmd.sunk | while | flops 201326592 | bytes 1311285 | solution.py:57
  163.1 3.5 collective-permute-start.2
  167.0 3.4 collective-permute-start.1
  170.4 3.7 collective-permute-done.2
  176.8 2.8 collective-permute-start.3
  179.6 7.2 collective-permute-done.4
  191.4 10.8 %collective-permute-done.6 = f32[256,256]{1,0:T(8,128)S(1)} collective-permute-done((f32[256,256]{1,0:T(8,128)S(1)}, f32[256,256]{1,0:T(8,128)S(1)}, u32[]{:S(2)}, u32[]{:S(2)}) %collective-permute-start.6) | collective-permute-done | bytes 262176 | tf_op jit(solution)/shard_map/ppermute | solution.py:12
  206.8 7.4 collective-permute-done.8
  218.2 7.4 collective-permute-done.10
  228.9 6.6 collective-permute-done.11
  235.6 21.4 %while.139 = (s32[]{:T(128)}, f32[32,256]{1,0:T(8,128)S(1)}, f32[16,32,256]{2,1,0:T(8,128)S(1)}, f32[16,256,256]{2,1,0:T(8,128)}, f32[16,32,256]{2,1,0:T(8,128)}, /*index=5*/s32[]{:T(128)}) while((s32[]{:T(128)}, f32[32,256]{1,0:T(8,128)S(1)}, f32[16,32,256]{2,1,0:T(8,128)S(1)}, f32[16,256,256]{2,1,0:T(8,128)}, f32[16,32,256]{2,1,0:T(8,128)}, ...), condition=%wide.region_5.6_spmd, body=%wide.region_4.5_spmd.sunk | while | flops 25174016 | bytes 459845 | solution.py:38
  257.0 21.3 %while.140 = (s32[]{:T(128)}, f32[32,256]{1,0:T(8,128)S(1)}, f32[16,32,256]{2,1,0:T(8,128)S(1)}, f32[16,256,256]{2,1,0:T(8,128)}, s32[]{:T(128)}, /*index=5*/s32[]{:T(128)}) while((s32[]{:T(128)}, f32[32,256]{1,0:T(8,128)S(1)}, f32[16,32,256]{2,1,0:T(8,128)S(1)}, f32[16,256,256]{2,1,0:T(8,128)}, s32[]{:T(128)}, /*index=5*/s32[]{:T(128)}) %tuple.283), condition=%wide.region_7.8_spmd, body=%wide.region_6.7_spmd.sunk | while | flops 25174020 | bytes 427089 | solution.py:48
  280.3 22.1 %while.141 = (s32[]{:T(128)}, f32[256,256]{1,0:T(8,128)S(1)}, f32[16,256,256]{2,1,0:T(8,128)}, s32[]{:T(128)}, s32[]{:T(128)}) while((s32[]{:T(128)}, f32[256,256]{1,0:T(8,128)S(1)}, f32[16,256,256]{2,1,0:T(8,128)}, s32[]{:T(128)}, s32[]{:T(128)}) %tuple.284), condition=%wide.region_9.10_spmd, body=%wide.region_8.9_spmd.sunk | while | flops 201326592 | bytes 1310797 | solution.py:57
  309.0 1.9 collective-permute-start.16
  311.8 4.5 collective-permute-start.15
  316.4 2.4 collective-permute-done.16
  319.2 1.9 collective-permute-start.18
  323.4 7.5 collective-permute-done.18
  331.2 2.2 collective-permute-start.20
  335.7 6.7 collective-permute-done.20
  342.8 2.1 collective-permute-start.22
  346.6 13.5 %collective-permute-done.22 = f32[256,256]{1,0:T(8,128)S(1)} collective-permute-done((f32[256,256]{1,0:T(8,128)S(1)}, f32[256,256]{1,0:T(8,128)S(1)}, u32[]{:S(2)}, u32[]{:S(2)}) %collective-permute-start.22) | collective-permute-done | bytes 262176 | tf_op jit(solution)/shard_map/ppermute | solution.py:12
  365.0 21.6 %while.142 = (s32[]{:T(128)}, f32[32,256]{1,0:T(8,128)S(1)}, f32[16,32,256]{2,1,0:T(8,128)S(1)}, f32[16,32,256]{2,1,0:T(8,128)}, f32[16,256,256]{2,1,0:T(8,128)}, /*index=5*/s32[]{:T(128)}, s32[]{:T(128)}) while((s32[]{:T(128)}, f32[32,256]{1,0:T(8,128)S(1)}, f32[16,32,256]{2,1,0:T(8,128)S(1)}, f32[16,32,256]{2,1,0:T(8,128)}, ...), condition=%wide.region_11.12_spmd, body=%wide.region_10.11_spmd.sunk | while | flops 25174020 | bytes 460377 | solution.py:48
  386.8 129.1 %psum.14 = f32[32]{0:T(128)S(1)} all-reduce(f32[32]{0:T(128)S(1)} %multiply_reduce_fusion.1), channel_id=1, replica_groups=mesh['chain'=64,'cols'=8] {'chain'}, use_global_device_ids=true, to_apply=%region_13.14 | all-reduce | flops 32 | bytes 256 | tf_op jit(solution)/shard_map/psum | solution.py:108
  516.9 21.5 %while.147 = (s32[]{:T(128)}, f32[32,256]{1,0:T(8,128)S(1)}, f32[16,256,256]{2,1,0:T(8,128)}, f32[16,32,256]{2,1,0:T(8,128)}, s32[]{:T(128)}, /*index=5*/s32[]{:T(128)}) while((s32[]{:T(128)}, f32[32,256]{1,0:T(8,128)S(1)}, f32[16,256,256]{2,1,0:T(8,128)}, f32[16,32,256]{2,1,0:T(8,128)}, s32[]{:T(128)}, ...), condition=%wide.region_15.16_spmd.clone, body=%wide.region_14.15_spmd.clone.sunk | while | flops 25182212 | bytes 427087 | solution.py:38
  540.3 6.6 collective-permute-done.24
  549.2 7.2 collective-permute-done.25
  556.7 2.1 collective-permute-start.26
  558.8 7.5 collective-permute-done.26
  568.6 5.1 collective-permute-done.27
  575.9 6.0 collective-permute-done.28
  583.6 8.4 collective-permute-done.29
  594.3 6.6 collective-permute-done.30
  600.9 21.4 %while.143 = (s32[]{:T(128)}, f32[32,256]{1,0:T(8,128)S(1)}, f32[16,32,256]{2,1,0:T(8,128)S(1)}, f32[16,256,256]{2,1,0:T(8,128)}, f32[16,32,256]{2,1,0:T(8,128)}, /*index=5*/s32[]{:T(128)}) while((s32[]{:T(128)}, f32[32,256]{1,0:T(8,128)S(1)}, f32[16,32,256]{2,1,0:T(8,128)S(1)}, f32[16,256,256]{2,1,0:T(8,128)}, f32[16,32,256]{2,1,0:T(8,128)}, ...), condition=%wide.region_17.18_spmd, body=%wide.region_16.17_spmd.sunk | while | flops 25174016 | bytes 459845 | solution.py:38
  622.4 21.3 %while.144 = (s32[]{:T(128)}, f32[32,256]{1,0:T(8,128)S(1)}, f32[16,32,256]{2,1,0:T(8,128)S(1)}, f32[16,256,256]{2,1,0:T(8,128)}, s32[]{:T(128)}, /*index=5*/s32[]{:T(128)}) while((s32[]{:T(128)}, f32[32,256]{1,0:T(8,128)S(1)}, f32[16,32,256]{2,1,0:T(8,128)S(1)}, f32[16,256,256]{2,1,0:T(8,128)}, s32[]{:T(128)}, /*index=5*/s32[]{:T(128)}) %tuple.288), condition=%wide.region_19.20_spmd, body=%wide.region_18.19_spmd.sunk | while | flops 25174020 | bytes 427089 | solution.py:48
  649.5 3.9 collective-permute-done.32
  655.6 5.4 collective-permute-done.33
  663.3 4.1 collective-permute-done.34
  669.6 4.8 collective-permute-done.35
  678.0 16.2 %collective-permute-start.37 = (f32[32,256]{1,0:T(8,128)S(1)}, f32[32,256]{1,0:T(8,128)S(1)}, u32[]{:S(2)}, u32[]{:S(2)}) collective-permute-start(f32[32,256]{1,0:T(8,128)S(1)} %convolution_add_fusion), channel_id=1, source_target_pairs={{8,0},{16,8},{24,16},{32,24},{40,32},{48,40},{56,48},{64,56},{72,6... | collective-permute-start | bytes 98312 | tf_op jit(solution)/shard_map/ppermute | solution.py:12
  695.9 21.3 %while.145 = (s32[]{:T(128)}, f32[32,256]{1,0:T(8,128)S(1)}, f32[16,32,256]{2,1,0:T(8,128)S(1)}, f32[16,32,256]{2,1,0:T(8,128)S(1)}, f32[16,256,256]{2,1,0:T(8,128)}, /*index=5*/s32[]{:T(128)}, s32[]{:T(128)}) while((s32[]{:T(128)}, f32[32,256]{1,0:T(8,128)S(1)}, f32[16,32,256]{2,1,0:T(8,128)S(1)}, f32[16,32,256]{2,1,0:T(8,128)S(1)}, ...), condition=%wide.region_21.22_spmd, body=%wide.region_20.21_spmd.sunk | while | flops 25174020 | bytes 460377 | solution.py:48
  717.3 129.1 %psum.15 = f32[32]{0:T(128)S(1)} all-reduce(f32[32]{0:T(128)S(1)} %multiply_reduce_fusion), channel_id=1, replica_groups=mesh['chain'=64,'cols'=8] {'chain'}, use_global_device_ids=true, to_apply=%region_23.24 | all-reduce | flops 32 | bytes 256 | tf_op jit(solution)/shard_map/psum | solution.py:113
  (421 shorter events, 286.3 us)
Async XLA Ops:
  4.5 106.6 %all-to-all-start = ((f32[16,256,256]{2,0,1:T(8,128)}), f32[16,256,256]{2,0,1:T(8,128)}, u32[]{:S(2)}, u32[]{:S(2)}) async-start(f32[16,256,256]{2,0,1:T(8,128)} %bitcast.211), calls=%async_computation | async-start | bytes 8388608 | tf_op jit(solution)/shard_map/all_to_all | solution.py:83
  139.0 27.5 %collective-permute-start = (f32[32,256]{1,0:T(8,128)S(1)}, f32[32,256]{1,0:T(8,128)S(1)}, u32[]{:S(2)}, u32[]{:S(2)}) collective-permute-start(f32[32,256]{1,0:T(8,128)S(1)} %get-tuple-element.568), channel_id=1, source_target_pairs={{0,8},{8,16},{16,24},{24,32},{32,40},{40,48},{48,56},{56,64},{64,7... | collective-permute-start | bytes 98312 | tf_op jit(solution)/shard_map/ppermute | solution.py:12
  163.1 11.0 %collective-permute-start.2 = (f32[256,256]{1,0:T(8,128)S(1)}, f32[256,256]{1,0:T(8,128)S(1)}, u32[]{:S(2)}, u32[]{:S(2)}) collective-permute-start(f32[256,256]{1,0:T(8,128)S(1)} %get-tuple-element.569), channel_id=1, source_target_pairs={{0,8},{8,16},{16,24},{24,32},{32,40},{40,48},{48,56},{56,64},{64,7... | collective-permute-start | bytes 786440 | tf_op jit(solution)/shard_map/ppermute | solution.py:12
  167.0 9.5 %collective-permute-start.1 = (f32[32,256]{1,0:T(8,128)S(1)}, f32[32,256]{1,0:T(8,128)S(1)}, u32[]{:S(2)}, u32[]{:S(2)}) collective-permute-start(f32[32,256]{1,0:T(8,128)S(1)} %convolution_add_fusion.23), channel_id=1, source_target_pairs={{0,16},{8,24},{16,32},{24,40},{32,48},{40,56},{48,64},{56,72},{64,... | collective-permute-start | bytes 98312 | tf_op jit(solution)/shard_map/ppermute | solution.py:12
  174.5 12.3 %collective-permute-start.4 = (f32[256,256]{1,0:T(8,128)S(1)}, f32[256,256]{1,0:T(8,128)S(1)}, u32[]{:S(2)}, u32[]{:S(2)}) collective-permute-start(f32[256,256]{1,0:T(8,128)S(1)} %fusion.54), channel_id=1, source_target_pairs={{0,16},{8,24},{16,32},{24,40},{32,48},{40,56},{48,64},{56,72},{64,... | collective-permute-start | bytes 786440 | tf_op jit(solution)/shard_map/ppermute | solution.py:12
  176.8 12.3 %collective-permute-start.3 = (f32[32,256]{1,0:T(8,128)S(1)}, f32[32,256]{1,0:T(8,128)S(1)}, u32[]{:S(2)}, u32[]{:S(2)}) collective-permute-start(f32[32,256]{1,0:T(8,128)S(1)} %convolution_add_fusion.22), channel_id=1, source_target_pairs={{0,32},{8,40},{16,48},{24,56},{32,64},{40,72},{48,80},{56,88},{64,... | collective-permute-start | bytes 98312 | tf_op jit(solution)/shard_map/ppermute | solution.py:12
  187.2 15.0 %collective-permute-start.6 = (f32[256,256]{1,0:T(8,128)S(1)}, f32[256,256]{1,0:T(8,128)S(1)}, u32[]{:S(2)}, u32[]{:S(2)}) collective-permute-start(f32[256,256]{1,0:T(8,128)S(1)} %fusion.55), channel_id=1, source_target_pairs={{0,32},{8,40},{16,48},{24,56},{32,64},{40,72},{48,80},{56,88},{64,... | collective-permute-start | bytes 786440 | tf_op jit(solution)/shard_map/ppermute | solution.py:12
  189.4 15.1 %collective-permute-start.5 = (f32[32,256]{1,0:T(8,128)S(1)}, f32[32,256]{1,0:T(8,128)S(1)}, u32[]{:S(2)}, u32[]{:S(2)}) collective-permute-start(f32[32,256]{1,0:T(8,128)S(1)} %convolution_add_fusion.21), channel_id=1, source_target_pairs={{0,64},{8,72},{16,80},{24,88},{32,96},{40,104},{48,112},{56,120},{... | collective-permute-start | bytes 98312 | tf_op jit(solution)/shard_map/ppermute | solution.py:12
  202.6 11.6 %collective-permute-start.8 = (f32[256,256]{1,0:T(8,128)S(1)}, f32[256,256]{1,0:T(8,128)S(1)}, u32[]{:S(2)}, u32[]{:S(2)}) collective-permute-start(f32[256,256]{1,0:T(8,128)S(1)} %fusion.56), channel_id=1, source_target_pairs={{0,64},{8,72},{16,80},{24,88},{32,96},{40,104},{48,112},{56,120},{... | collective-permute-start | bytes 786440 | tf_op jit(solution)/shard_map/ppermute | solution.py:12
  204.9 11.7 %collective-permute-start.7 = (f32[32,256]{1,0:T(8,128)S(1)}, f32[32,256]{1,0:T(8,128)S(1)}, u32[]{:S(2)}, u32[]{:S(2)}) collective-permute-start(f32[32,256]{1,0:T(8,128)S(1)} %convolution_add_fusion.20), channel_id=1, source_target_pairs={{0,128},{8,136},{16,144},{24,152},{32,160},{40,168},{48,176},{56,1... | collective-permute-start | bytes 98312 | tf_op jit(solution)/shard_map/ppermute | solution.py:12
  214.6 11.0 %collective-permute-start.10 = (f32[256,256]{1,0:T(8,128)S(1)}, f32[256,256]{1,0:T(8,128)S(1)}, u32[]{:S(2)}, u32[]{:S(2)}) collective-permute-start(f32[256,256]{1,0:T(8,128)S(1)} %fusion.57), channel_id=1, source_target_pairs={{0,128},{8,136},{16,144},{24,152},{32,160},{40,168},{48,176},{56,1... | collective-permute-start | bytes 786440 | tf_op jit(solution)/shard_map/ppermute | solution.py:12
  216.9 9.7 %collective-permute-start.9 = (f32[32,256]{1,0:T(8,128)S(1)}, f32[32,256]{1,0:T(8,128)S(1)}, u32[]{:S(2)}, u32[]{:S(2)}) collective-permute-start(f32[32,256]{1,0:T(8,128)S(1)} %convolution_add_fusion.19), channel_id=1, source_target_pairs={{0,256},{8,264},{16,272},{24,280},{32,288},{40,296},{48,304},{56,3... | collective-permute-start | bytes 98312 | tf_op jit(solution)/shard_map/ppermute | solution.py:12
  227.0 8.6 %collective-permute-start.11 = (f32[32,256]{1,0:T(8,128)S(1)}, f32[32,256]{1,0:T(8,128)S(1)}, u32[]{:S(2)}, u32[]{:S(2)}) collective-permute-start(f32[32,256]{1,0:T(8,128)S(1)} %convolution_add_fusion.18), channel_id=1, source_target_pairs={{0,8},{8,16},{16,24},{24,32},{32,40},{40,48},{48,56},{56,64},{64,7... | collective-permute-start | bytes 98312 | tf_op jit(solution)/shard_map/ppermute | solution.py:12
  278.3 28.3 %copy-start.2 = (f32[16,32,256]{2,1,0:T(8,128)}, f32[16,32,256]{2,1,0:T(8,128)S(1)}, u32[]{:S(2)}) copy-start(f32[16,32,256]{2,1,0:T(8,128)S(1)} %get-tuple-element.1222) | copy-start | bytes 1572868
  278.4 26.0 %collective-permute-start.12 = (f32[32,256]{1,0:T(8,128)S(1)}, f32[32,256]{1,0:T(8,128)S(1)}, u32[]{:S(2)}, u32[]{:S(2)}) collective-permute-start(f32[32,256]{1,0:T(8,128)S(1)} %get-tuple-element.571), channel_id=1, source_target_pairs={{8,0},{16,8},{24,16},{32,24},{40,32},{48,40},{56,48},{64,56},{72,6... | collective-permute-start | bytes 98312 | tf_op jit(solution)/shard_map/ppermute | solution.py:12
  302.4 6.1 collective-permute-start.14
  304.7 6.8 collective-permute-start.13
  309.0 9.8 %collective-permute-start.16 = (f32[256,256]{1,0:T(8,128)S(1)}, f32[256,256]{1,0:T(8,128)S(1)}, u32[]{:S(2)}, u32[]{:S(2)}) collective-permute-start(f32[256,256]{1,0:T(8,128)S(1)} %fusion.59), channel_id=1, source_target_pairs={{16,0},{24,8},{32,16},{40,24},{48,32},{56,40},{64,48},{72,56},{80,... | collective-permute-start | bytes 786440 | tf_op jit(solution)/shard_map/ppermute | solution.py:12
  311.8 9.2 %collective-permute-start.15 = (f32[32,256]{1,0:T(8,128)S(1)}, f32[32,256]{1,0:T(8,128)S(1)}, u32[]{:S(2)}, u32[]{:S(2)}) collective-permute-start(f32[32,256]{1,0:T(8,128)S(1)} %convolution_add_fusion.16), channel_id=1, source_target_pairs={{32,0},{40,8},{48,16},{56,24},{64,32},{72,40},{80,48},{88,56},{96,... | collective-permute-start | bytes 98312 | tf_op jit(solution)/shard_map/ppermute | solution.py:12
  319.2 11.7 %collective-permute-start.18 = (f32[256,256]{1,0:T(8,128)S(1)}, f32[256,256]{1,0:T(8,128)S(1)}, u32[]{:S(2)}, u32[]{:S(2)}) collective-permute-start(f32[256,256]{1,0:T(8,128)S(1)} %fusion.60), channel_id=1, source_target_pairs={{32,0},{40,8},{48,16},{56,24},{64,32},{72,40},{80,48},{88,56},{96,... | collective-permute-start | bytes 786440 | tf_op jit(solution)/shard_map/ppermute | solution.py:12
  321.4 12.0 %collective-permute-start.17 = (f32[32,256]{1,0:T(8,128)S(1)}, f32[32,256]{1,0:T(8,128)S(1)}, u32[]{:S(2)}, u32[]{:S(2)}) collective-permute-start(f32[32,256]{1,0:T(8,128)S(1)} %convolution_add_fusion.15), channel_id=1, source_target_pairs={{64,0},{72,8},{80,16},{88,24},{96,32},{104,40},{112,48},{120,56},{... | collective-permute-start | bytes 98312 | tf_op jit(solution)/shard_map/ppermute | solution.py:12
  331.2 11.2 %collective-permute-start.20 = (f32[256,256]{1,0:T(8,128)S(1)}, f32[256,256]{1,0:T(8,128)S(1)}, u32[]{:S(2)}, u32[]{:S(2)}) collective-permute-start(f32[256,256]{1,0:T(8,128)S(1)} %fusion.61), channel_id=1, source_target_pairs={{64,0},{72,8},{80,16},{88,24},{96,32},{104,40},{112,48},{120,56},{... | collective-permute-start | bytes 786440 | tf_op jit(solution)/shard_map/ppermute | solution.py:12
  333.8 11.1 %collective-permute-start.19 = (f32[32,256]{1,0:T(8,128)S(1)}, f32[32,256]{1,0:T(8,128)S(1)}, u32[]{:S(2)}, u32[]{:S(2)}) collective-permute-start(f32[32,256]{1,0:T(8,128)S(1)} %convolution_add_fusion.14), channel_id=1, source_target_pairs={{128,0},{136,8},{144,16},{152,24},{160,32},{168,40},{176,48},{184,... | collective-permute-start | bytes 98312 | tf_op jit(solution)/shard_map/ppermute | solution.py:12
  342.8 17.2 %collective-permute-start.22 = (f32[256,256]{1,0:T(8,128)S(1)}, f32[256,256]{1,0:T(8,128)S(1)}, u32[]{:S(2)}, u32[]{:S(2)}) collective-permute-start(f32[256,256]{1,0:T(8,128)S(1)} %fusion.62), channel_id=1, source_target_pairs={{128,0},{136,8},{144,16},{152,24},{160,32},{168,40},{176,48},{184,... | collective-permute-start | bytes 786440 | tf_op jit(solution)/shard_map/ppermute | solution.py:12
  345.3 15.2 %collective-permute-start.21 = (f32[32,256]{1,0:T(8,128)S(1)}, f32[32,256]{1,0:T(8,128)S(1)}, u32[]{:S(2)}, u32[]{:S(2)}) collective-permute-start(f32[32,256]{1,0:T(8,128)S(1)} %convolution_add_fusion.13), channel_id=1, source_target_pairs={{256,0},{264,8},{272,16},{280,24},{288,32},{296,40},{304,48},{312,... | collective-permute-start | bytes 98312 | tf_op jit(solution)/shard_map/ppermute | solution.py:12
  360.4 0.7 copy-start
  361.5 3.5 collective-permute-start.23
  538.4 8.6 %collective-permute-start.24 = (f32[32,256]{1,0:T(8,128)S(1)}, f32[32,256]{1,0:T(8,128)S(1)}, u32[]{:S(2)}, u32[]{:S(2)}) collective-permute-start(f32[32,256]{1,0:T(8,128)S(1)} %get-tuple-element.574), channel_id=1, source_target_pairs={{0,8},{8,16},{16,24},{24,32},{32,40},{40,48},{48,56},{56,64},{64,7... | collective-permute-start | bytes 98312 | tf_op jit(solution)/shard_map/ppermute | solution.py:12
  547.3 9.1 %collective-permute-start.25 = (f32[32,256]{1,0:T(8,128)S(1)}, f32[32,256]{1,0:T(8,128)S(1)}, u32[]{:S(2)}, u32[]{:S(2)}) collective-permute-start(f32[32,256]{1,0:T(8,128)S(1)} %convolution_add_fusion.11), channel_id=1, source_target_pairs={{0,16},{8,24},{16,32},{24,40},{32,48},{40,56},{48,64},{56,72},{64,... | collective-permute-start | bytes 98312 | tf_op jit(solution)/shard_map/ppermute | solution.py:12
  556.7 120.9 %copy-start.1 = (f32[256,256]{1,0:T(8,128)S(1)}, f32[256,256]{1,0:T(8,128)}, u32[]{:S(2)}) copy-start(f32[256,256]{1,0:T(8,128)} %copy-done) | copy-start | bytes 786436
  556.7 9.6 %collective-permute-start.26 = (f32[32,256]{1,0:T(8,128)S(1)}, f32[32,256]{1,0:T(8,128)S(1)}, u32[]{:S(2)}, u32[]{:S(2)}) collective-permute-start(f32[32,256]{1,0:T(8,128)S(1)} %convolution_add_fusion.10), channel_id=1, source_target_pairs={{0,32},{8,40},{16,48},{24,56},{32,64},{40,72},{48,80},{56,88},{64,... | collective-permute-start | bytes 98312 | tf_op jit(solution)/shard_map/ppermute | solution.py:12
  566.6 7.0 collective-permute-start.27
  574.0 7.9 collective-permute-start.28
  582.3 9.7 %collective-permute-start.29 = (f32[32,256]{1,0:T(8,128)S(1)}, f32[32,256]{1,0:T(8,128)S(1)}, u32[]{:S(2)}, u32[]{:S(2)}) collective-permute-start(f32[32,256]{1,0:T(8,128)S(1)} %convolution_add_fusion.7), channel_id=1, source_target_pairs={{0,256},{8,264},{16,272},{24,280},{32,288},{40,296},{48,304},{56,3... | collective-permute-start | bytes 98312 | tf_op jit(solution)/shard_map/ppermute | solution.py:12
  592.3 8.6 %collective-permute-start.30 = (f32[32,256]{1,0:T(8,128)S(1)}, f32[32,256]{1,0:T(8,128)S(1)}, u32[]{:S(2)}, u32[]{:S(2)}) collective-permute-start(f32[32,256]{1,0:T(8,128)S(1)} %convolution_add_fusion.6), channel_id=1, source_target_pairs={{0,8},{8,16},{16,24},{24,32},{32,40},{40,48},{48,56},{56,64},{64,7... | collective-permute-start | bytes 98312 | tf_op jit(solution)/shard_map/ppermute | solution.py:12
  643.7 3.5 collective-permute-start.31
  647.5 5.8 collective-permute-start.32
  653.7 7.3 collective-permute-start.33
  661.4 6.0 collective-permute-start.34
  667.7 6.7 collective-permute-start.35
  674.8 2.9 collective-permute-start.36
  678.0 17.8 %collective-permute-start.37 = (f32[32,256]{1,0:T(8,128)S(1)}, f32[32,256]{1,0:T(8,128)S(1)}, u32[]{:S(2)}, u32[]{:S(2)}) collective-permute-start(f32[32,256]{1,0:T(8,128)S(1)} %convolution_add_fusion), channel_id=1, source_target_pairs={{8,0},{16,8},{24,16},{32,24},{40,32},{48,40},{56,48},{64,56},{72,6... | collective-permute-start | bytes 98312 | tf_op jit(solution)/shard_map/ppermute | solution.py:12
